TPU v7x, 128 devices: a whole 4x4x4 slice. The times are simulated.
128 devices in a mesh: section: 32 (over y, x, z_lo), tensor: 4 (over z_hi, core).
Axes of the slice: x: 4, y: 4, z: 4 (z_hi: 2, z_lo: 2; z = z_hi * 2 + z_lo), core: 2. Of those that a mesh axis runs over, the one named last changes fastest.
Arguments:
- weights: bfloat16 [32, 4096, 4096], P('section', 'tensor'), may hold values from -0.09375 to 0.09375
- filters: float32 [32, 32, 128], P('section'), may hold values from -0.5 to 0.5
- down_input: bfloat16 [32, 512, 4096], P('section', 'tensor'), may hold values from -6 to 6
- down_cot: bfloat16 [32, 512, 4096], P('section', 'tensor'), may hold values from -6 to 6
- up_input: bfloat16 [32, 512, 4096], P('section', 'tensor'), may hold values from -6 to 6
- up_cot: bfloat16 [32, 512, 4096], P('section', 'tensor'), may hold values from -6 to 6
Outputs:
- weight_grad: bfloat16 [32, 4096, 4096], P('section', 'tensor')
- filter_grad: float32 [32, 32, 128], P('section')
- down_passed: bfloat16 [32, 512, 4096], P('section', 'tensor')
- up_passed: bfloat16 [32, 512, 4096], P('section', 'tensor')
All inputs are finite; a program needn't handle non-finite values.
Results may differ from a plain program's by a relative error of at most 0.014.
Values may be sent and summed in bfloat16 or wider, within the bound.
A program may use at most 192 MiB of HBM per device.

v0:
```python
import jax
import jax.numpy as jnp
from jax import lax
from jax.sharding import PartitionSpec as P

epsilon = 1e-06


def shifted(x, axis, by):
    devices = lax.axis_size(axis)
    pairs = [(i, i + by) for i in range(devices) if 0 <= i + by < devices]
    return lax.ppermute(x, axis, pairs)


def tap_tables(row_count, taps_total):
    target = jnp.arange(row_count, dtype=jnp.int32)[:, None, None]
    source = jnp.arange(row_count + taps_total - 1, dtype=jnp.int32)[None, :, None]
    lag_index = jnp.arange(taps_total, dtype=jnp.int32)[None, None, :]
    causal_table = (target + taps_total - 1 - source == lag_index).astype(jnp.float32)
    ahead_table = (source - target == lag_index).astype(jnp.float32)
    return (causal_table, ahead_table)


def banded(table, filter_taps, extended, row_count):
    group_count = filter_taps.shape[0]
    band = jnp.einsum("tuk,gk->gtu", table, filter_taps, precision=lax.Precision.HIGHEST)
    grouped = extended.reshape(extended.shape[0], extended.shape[1], group_count, -1)
    mixed_out = jnp.einsum("gtu,umgc->tmgc", band, grouped, precision=lax.Precision.HIGHEST)
    return mixed_out.reshape(row_count, extended.shape[1], extended.shape[2])


def layer_grads(inputs, cotangent, weight_rows, filter_taps, tables):
    causal_table, ahead_table = tables
    row_count = inputs.shape[0]
    group_count = filter_taps.shape[0]
    taps_total = filter_taps.shape[1]
    input_wide = inputs.astype(jnp.float32)
    inverse_rms = lax.rsqrt(jnp.mean(input_wide * input_wide, axis=2, keepdims=True) + epsilon)
    normed = input_wide * inverse_rms
    normed_b = normed.astype(jnp.bfloat16)
    feature_rows = lax.all_to_all(normed_b, "tensor", split_axis=2, concat_axis=0, tiled=True)
    selected = feature_rows
    values = lax.psum_scatter(
        jnp.einsum("tmd,de->tme", selected, weight_rows, preferred_element_type=jnp.float32).astype(
            jnp.bfloat16
        ),
        "tensor",
        scatter_dimension=0,
        tiled=True,
    ).astype(jnp.float32)
    before = shifted(
        values[row_count - (taps_total - 1) :].astype(jnp.bfloat16), "tensor", 1
    ).astype(jnp.float32)
    extended = jnp.concatenate([before, values], axis=0)
    convolved = banded(causal_table, filter_taps, extended, row_count)
    cot_wide = cotangent.astype(jnp.float32)
    grad_mix = cot_wide * normed
    following = shifted(grad_mix[: taps_total - 1], "tensor", -1)
    grad_ext = jnp.concatenate([grad_mix, following], axis=0)
    grad_values = banded(ahead_table, filter_taps, grad_ext, row_count)
    grad_grouped = grad_mix.reshape(row_count, grad_mix.shape[1], group_count, -1)
    ext_grouped = extended.reshape(extended.shape[0], extended.shape[1], group_count, -1)
    pairs = jnp.einsum("tmgc,umgc->gtu", grad_grouped, ext_grouped, precision=lax.Precision.HIGHEST)
    tap_part = jnp.einsum("gtu,tuk->gk", pairs, causal_table, precision=lax.Precision.HIGHEST)
    grad_values_b = grad_values.astype(jnp.bfloat16)
    shard_rows = lax.all_gather(grad_values_b, "tensor", axis=0, tiled=True)
    selected = feature_rows
    weight_sum = jnp.einsum("tmd,tme->de", selected, shard_rows, preferred_element_type=jnp.float32)
    returned_rows = jnp.einsum(
        "tme,de->tmd", shard_rows, weight_rows, preferred_element_type=jnp.float32
    )
    back_tokens = lax.all_to_all(
        returned_rows.astype(jnp.bfloat16), "tensor", split_axis=0, concat_axis=2, tiled=True
    ).astype(returned_rows.dtype)
    grad_total = cot_wide * convolved + back_tokens
    projection_mean = jnp.mean(grad_total * normed, axis=2, keepdims=True)
    grad_in = (cot_wide + inverse_rms * (grad_total - normed * projection_mean)).astype(
        jnp.bfloat16
    )
    return (grad_in, weight_sum, tap_part)


def mirrored(stacked):
    sections = lax.axis_size("section")
    pieces = stacked.reshape(
        stacked.shape[0], stacked.shape[1], sections, stacked.shape[2] // sections
    )
    spread = lax.all_to_all(pieces, "section", split_axis=2, concat_axis=2, tiled=True)
    collected = lax.all_to_all(
        jnp.flip(spread, 2), "section", split_axis=2, concat_axis=2, tiled=True
    )
    return collected.reshape(stacked.shape)


def per_device(weights, filters, down_input, down_cot, up_input, up_cot):
    weight_rows = weights[0]
    filter_taps = filters[0]
    tables = tap_tables(down_input.shape[1], filter_taps.shape[1])
    arriving = mirrored(jnp.stack([up_input[0], up_cot[0]], axis=1))
    up_inputs = arriving[:, 0:1]
    up_cotangent = arriving[:, 1:2]
    down_inputs = down_input[0][:, None]
    down_cotangent = down_cot[0][:, None]
    down_result, down_weight, down_taps = layer_grads(
        down_inputs, down_cotangent, weight_rows, filter_taps, tables
    )
    up_grad, up_weight, up_taps = layer_grads(
        up_inputs, up_cotangent, weight_rows, filter_taps, tables
    )
    down_grad = down_result[:, 0]
    weight_part = down_weight + up_weight
    tap_part = down_taps + up_taps
    taps_total = lax.psum(tap_part, "tensor")
    down_passed = shifted(down_grad, "section", -1)
    up_passed = shifted(mirrored(up_grad)[:, 0], "section", 1)
    return (
        weight_part.astype(jnp.bfloat16)[None],
        taps_total[None],
        down_passed[None],
        up_passed[None],
    )


def solution(mesh):
    in_specs = (
        P("section", "tensor", None),
        P("section", None, None),
        P("section", "tensor", None),
        P("section", "tensor", None),
        P("section", "tensor", None),
        P("section", "tensor", None),
    )
    out_specs = (
        P("section", "tensor", None),
        P("section", None, None),
        P("section", "tensor", None),
        P("section", "tensor", None),
    )
    return jax.shard_map(
        per_device, mesh=mesh, in_specs=in_specs, out_specs=out_specs, check_vma=False
    )
```

profile of v0, /device:TPU:0, one launch (start us, length us, event | category | flops | bytes accessed | tf_op | source)
XLA Modules:
  0.0 634.0 jit_solution(15924524114291938445)
XLA Ops:
  9.6 3.3 fusion.89
  13.4 23.4 %reduce.5 = bf16[4096,128]{1,0:T(8,128)(2,1)} reduce(bf16[4096,1,128]{2,1,0:T(2,128)(2,1)S(1)} %bitcast.223, bf16[]{:T(256)} %broadcast.137), dimensions={1}, to_apply=%bitcast.182.reduce_sub_computation | reduce | bytes 2097154
  39.0 21.1 %all_to_all.68 = bf16[4,2,65536]{2,1,0:T(2,128)(2,1)} all-to-all(bf16[4,2,65536]{2,1,0:T(2,128)(2,1)S(1)} %reshape.472), channel_id=1, replica_groups=mesh['section'=32,'tensor'=4] {'tensor'}, dimensions={0} | all-to-all | bytes 2097152 | tf_op jit(solution)/shard_map/all_to_all | solution.py:41
  60.1 2.6 reshape.473
  65.3 9.8 %fusion.26 = bf16[512,1,4096]{2,0,1:T(8,128)(2,1)} fusion(bf16[512,1024]{1,0:T(8,128)(2,1)S(1)} %bitcast.238, bf16[1,1024,4096]{2,1,0:T(8,128)(2,1)} %param.6), kind=kOutput, calls=%fused_computation.23 | convolution fusion | flops 4297064448 | bytes 13631488 | tf_op jit(solution)/shard_map/tmd,de->tme/dot_general | solution.py:44
  82.3 6.6 %copy.99 = f32[127,1,4096]{2,1,0:T(1,128)} copy(f32[127,1,4096]{0,1,2:T(1,128)S(1)} %slice_multiply_fusion) | data formatting | bytes 4161536 | tf_op jit(solution)/shard_map/slice | solution.py:58
  95.0 7.8 %all-to-all-start.1 = ((bf16[128,2,32,128]{0,3,1,2:T(8,128)(2,1)}), bf16[128,2,32,128]{0,3,1,2:T(8,128)(2,1)S(1)}, u32[]{:S(2)}, u32[]{:S(2)}) async-start(bf16[128,2,32,128]{0,3,1,2:T(8,128)(2,1)} %pad_maximum_fusion.1), calls=%async_computation.1 | async-start | bytes 4194304 | tf_op jit(solution)/shard_map/all_to_all | solution.py:88
  102.8 11.5 %all-gather.3.cloned.1.call-start = ((), (), s32[]{:S(2)}) async-start(), calls=%async_computation.10 | async-start | bytes 5242880 | tf_op jit(solution)/shard_map/all_gather | solution.py:66
  114.3 14.0 %fusion.40 = f32[32,128,255]{1,0,2:T(8,128)} fusion(s32[128,255]{0,1:T(8,128)S(1)} %iota_subtract_fusion.1, f32[1,32,128]{2,1,0:T(8,128)S(1)} %copy-done), kind=kOutput, calls=%fused_computation.42 | convolution fusion | flops 1608499200 | bytes 4324864 | tf_op jit(solution)/shard_map/tuk,gk->gtu/dot_general | solution.py:26
  128.3 5.2 copy.101
  133.6 5.7 copy.100
  139.3 8.7 %fusion.60 = bf16[32,128,128]{2,1,0:T(8,128)(2,1)} fusion(f32[32,128,255]{2,1,0:T(8,128)} %copy.101, f32[127,1,32,128]{0,3,2,1:T(8,128)} %bitcast.229, f32[128,1,32,128]{0,3,2,1:T(8,128)} %get-tuple-element.16), kind=kOutput, calls=%fused_computation.72 | convolution fusion | flops 1605890048 | bytes 9404416 | tf_op jit(solution)/shard_map/gtu,umgc->tmgc/dot_general | solution.py:28
  149.5 27.6 %all_to_all.69 = bf16[128,2,32,128]{0,3,1,2:T(8,128)(2,1)S(1)} all-to-all(bf16[128,2,32,128]{0,3,1,2:T(8,128)(2,1)} %rev.8), channel_id=1, replica_groups=mesh['section'=32,'tensor'=4] {'section'}, dimensions={2} | all-to-all | bytes 4194304 | tf_op jit(solution)/shard_map/all_to_all | solution.py:89
  179.6 17.0 %copy.134 = bf16[128,1,4096]{0,1,2:T(2,128)(2,1)} copy(bf16[128,1,4096]{0,2,1:T(8,128)(2,1)S(1)} %get-tuple-element.21) | data formatting | bytes 2097152 | tf_op jit(solution)/shard_map/convert_element_type | solution.py:40
  196.6 24.5 %reduce.6 = bf16[4096,128]{1,0:T(8,128)(2,1)} reduce(bf16[4096,1,128]{2,1,0:T(2,128)(2,1)} %bitcast.226, bf16[]{:T(256)} %broadcast.137), dimensions={1}, to_apply=%bitcast.203.reduce_sub_computation | reduce | bytes 2097154
  221.1 3.5 reshape.474
  224.6 55.9 %all_to_all.70 = bf16[4,2,65536]{2,1,0:T(2,128)(2,1)} all-to-all(bf16[4,2,65536]{2,1,0:T(2,128)(2,1)} %reshape.474), channel_id=1, replica_groups=mesh['section'=32,'tensor'=4] {'tensor'}, dimensions={0} | all-to-all | bytes 2097152 | tf_op jit(solution)/shard_map/all_to_all | solution.py:41
  280.5 4.0 reshape.475
  284.5 2.7 copy.130
  289.5 10.2 %fusion.23 = bf16[512,1,4096]{2,0,1:T(8,128)(2,1)} fusion(bf16[512,1024]{1,0:T(8,128)(2,1)} %bitcast.240, bf16[1,1024,4096]{2,1,0:T(8,128)(2,1)} %param.6), kind=kOutput, calls=%fused_computation.22 | convolution fusion | flops 4297064448 | bytes 13631488 | tf_op jit(solution)/shard_map/tmd,de->tme/dot_general | solution.py:44
  299.7 5.7 copy.107
  306.8 5.1 collective-permute-done.1
  311.9 5.7 copy.108
  317.5 2.7 pad_maximum_fusion
  321.3 5.2 convolution_convert_fusion
  329.1 44.7 %collective-permute-start.2 = (bf16[127,1,4096]{2,0,1:T(8,128)(2,1)}, bf16[127,1,4096]{2,0,1:T(8,128)(2,1)}, u32[]{:S(2)}, u32[]{:S(2)}) collective-permute-start(bf16[127,1,4096]{2,0,1:T(8,128)(2,1)} %slice.31), channel_id=1, source_target_pairs={{0,1},{1,2},{2,3},{4,5},{5,6},{6,7},{8,9},{9,10},{10,11},{12,13},{... | collective-permute-start | bytes 3121160 | tf_op jit(solution)/shard_map/ppermute | solution.py:12
  373.8 10.4 %fusion.76 = bf16[512,1,1024]{2,0,1:T(8,128)(2,1)} fusion(bf16[1,1024,4096]{2,1,0:T(8,128)(2,1)} %param.6, bf16[512,1,4096]{0,2,1:T(8,128)(2,1)} %all-gather.3.cloned.1.call-done), kind=kOutput, calls=%fused_computation.77 | convolution fusion | flops 4295491584 | bytes 13631488 | tf_op jit(solution)/shard_map/tme,de->tmd/dot_general | solution.py:69
  384.2 3.3 reduce.7
  387.5 3.7 reshape.476
  391.2 4.2 all-to-all-start.4
  395.5 14.0 %fusion.41 = f32[32,128,255]{1,0,2:T(8,128)} fusion(s32[128,255]{0,1:T(8,128)S(1)} %iota_subtract_fusion, f32[1,32,128]{2,1,0:T(8,128)S(1)} %copy-done), kind=kOutput, calls=%fused_computation.43 | convolution fusion | flops 1608499200 | bytes 4324864 | tf_op jit(solution)/shard_map/tuk,gk->gtu/dot_general | solution.py:26
  409.4 5.2 copy.118
  414.7 2.9 copy.111
  417.6 2.9 copy.110
  420.5 4.0 reshape.477
  424.5 6.1 copy.120
  430.6 3.2 pad_maximum_fusion.2
  433.8 4.1 copy.131
  440.3 3.3 collective-permute-start.3
  443.7 10.2 %fusion.71 = bf16[512,1,1024]{2,0,1:T(8,128)(2,1)} fusion(bf16[1,1024,4096]{2,1,0:T(8,128)(2,1)} %param.6, bf16[512,1,4096]{0,2,1:T(8,128)(2,1)} %all-gather.5.cloned.1.call-done), kind=kOutput, calls=%fused_computation.76 | convolution fusion | flops 4295491584 | bytes 13631488 | tf_op jit(solution)/shard_map/tme,de->tmd/dot_general | solution.py:69
  453.8 3.4 reduce.8
  457.2 3.7 reshape.478
  460.9 4.5 all-to-all-start.5
  465.4 8.6 %fusion.54 = (f32[128]{0:T(128)S(1)}, f32[32,128,128]{2,1,0:T(8,128)}) fusion(f32[128,1,32,128]{0,3,2,1:T(8,128)} %bitcast.221, f32[128,1,32,128]{0,3,2,1:T(8,128)} %bitcast.211, f32[128,1,32,128]{0,3,2,1:T(8,128)} %bitcast.214, f32[128]{0:T(128)S(1)} %add_rsqrt_fusion.1, bf16[255,32,128]{0,2,1:T(8,128)(2,1)} %bitcast.219, f32[32,128,255]{2,1,0:T(8,128)} %copy.118), kind=kOutput, calls=%fused_computation.63 | convolution fusion | flops 1606942592 | bytes 14656512 | tf_op jit(solution)/shard_map/gtu,umgc->tmgc/dot_general | solution.py:28
  474.0 7.4 %all-to-all-done.5 = bf16[4,2,65536]{2,1,0:T(2,128)(2,1)} async-done(((bf16[4,2,65536]{2,1,0:T(2,128)(2,1)}), bf16[4,2,65536]{2,1,0:T(2,128)(2,1)}, u32[]{:S(2)}, u32[]{:S(2)}) %all-to-all-start.5) | async-done | bytes 1048608 | tf_op jit(solution)/shard_map/all_to_all | solution.py:72
  481.4 4.0 reshape.479
  485.4 6.1 copy.124
  491.5 3.2 pad_maximum_fusion.3
  494.7 4.1 copy.132
  498.8 5.3 fusion.91
  506.3 4.8 all-to-all-start.6
  511.1 3.8 fusion.51
  516.3 12.8 %all-to-all-done.6 = bf16[128,1,32,128]{0,3,1,2:T(8,128)(2,1)} async-done(((bf16[128,1,32,128]{0,3,1,2:T(8,128)(2,1)}), bf16[128,1,32,128]{0,3,1,2:T(8,128)(2,1)}, u32[]{:S(2)}, u32[]{:S(2)}) %all-to-all-start.6) | async-done | bytes 1048608 | tf_op jit(solution)/shard_map/all_to_all | solution.py:88
  531.4 5.5 all-to-all-start.7
  536.9 10.5 %fusion.35 = f32[1024,4096]{1,0:T(8,128)} fusion(bf16[512,1024]{1,0:T(8,128)(2,1)S(1)} %bitcast.239, bf16[512,1,4096]{0,2,1:T(8,128)(2,1)} %all-gather.3.cloned.1.call-done), kind=kOutput, calls=%fused_computation.32 | convolution fusion | flops 4294967296 | bytes 22020096 | tf_op jit(solution)/shard_map/tmd,tme->de/dot_general | solution.py:68
  547.5 3.9 fusion.57
  551.4 5.5 copy.113
  556.8 11.2 %fusion.81 = f32[32,128]{1,0:T(8,128)S(1)} fusion(f32[32,128,255]{1,0,2:T(8,128)} %copy.113, s32[128,255]{0,1:T(8,128)S(1)} %iota_subtract_fusion), kind=kOutput, calls=%fused_computation.78 | convolution fusion | flops 1608499200 | bytes 4324864 | tf_op jit(solution)/shard_map/gtu,tuk->gk/dot_general | solution.py:64
  572.6 4.9 collective-permute-start.5
  577.5 11.4 %fusion.4 = bf16[1,1024,4096]{2,1,0:T(8,128)(2,1)} fusion(f32[1024,4096]{1,0:T(8,128)} %fusion.35, bf16[512,1024]{1,0:T(8,128)(2,1)S(1)} %bitcast.241, bf16[512,1,4096]{0,2,1:T(8,128)(2,1)} %all-gather.5.cloned.1.call-done), kind=kOutput, calls=%fused_computation.7 | convolution fusion | flops 4303355904 | bytes 30408704 | tf_op jit(solution)/shard_map/tmd,tme->de/dot_general | solution.py:68
  589.0 5.4 fusion.90
  594.4 5.5 copy.116
  599.8 11.2 %fusion.84 = f32[1,32,128]{2,1,0:T(8,128)S(1)} fusion(f32[32,128]{1,0:T(8,128)S(1)} %fusion.81, f32[32,128,255]{1,0,2:T(8,128)} %copy.116, s32[128,255]{0,1:T(8,128)S(1)} %iota_subtract_fusion), kind=kOutput, calls=%fused_computation.81 | convolution fusion | flops 1608503296 | bytes 4341248 | tf_op jit(solution)/shard_map/gtu,tuk->gk/dot_general | solution.py:64
  611.0 13.7 %psum.7 = f32[1,32,128]{2,1,0:T(8,128)} all-reduce(f32[1,32,128]{2,1,0:T(8,128)S(1)} %fusion.84), channel_id=1, replica_groups=mesh['section'=32,'tensor'=4] {'tensor'}, use_global_device_ids=true, to_apply=%region_4.5 | all-reduce | flops 4096 | bytes 32768 | tf_op jit(solution)/shard_map/psum | solution.py:113
  (91 shorter events, 47.5 us)
Async XLA Ops:
  7.2 107.2 %copy-start = (f32[1,32,128]{2,1,0:T(8,128)S(1)}, f32[1,32,128]{2,1,0:T(8,128)}, u32[]{:S(2)}) copy-start(f32[1,32,128]{2,1,0:T(8,128)} %param.7) | copy-start | bytes 49156
  7.2 319.4 %reduce-scatter.3.cloned.1.call-start = ((), (), s32[]{:S(2)}) async-start(), calls=%async_computation.12 | async-start | bytes 5242880 | tf_op jit(solution)/shard_map/reduce_scatter | solution.py:43
  9.5 3.4 copy-start.4
  65.3 9.8 %copy-start.14 = (bf16[4,128,1,1024]{3,1,0,2:T(8,128)(2,1)}, bf16[4,128,1,1024]{3,1,0,2:T(8,128)(2,1)S(1)}, u32[]{:S(2)}) copy-start(bf16[4,128,1,1024]{3,1,0,2:T(8,128)(2,1)S(1)} %copy.97) | copy-start | bytes 3145732
  75.1 1.2 copy-start.13
  77.0 1.8 copy-start.9
  77.0 3.1 copy-start.10
  78.8 1.3 copy-start.3
  89.0 44.6 %collective-permute-start = (f32[127,1,4096]{2,1,0:T(1,128)}, f32[127,1,4096]{2,1,0:T(1,128)}, u32[]{:S(2)}, u32[]{:S(2)}) collective-permute-start(f32[127,1,4096]{2,1,0:T(1,128)} %copy.99), channel_id=1, source_target_pairs={{1,0},{2,1},{3,2},{5,4},{6,5},{7,6},{9,8},{10,9},{11,10},{13,12},{... | collective-permute-start | bytes 6242312 | tf_op jit(solution)/shard_map/ppermute | solution.py:12
  95.0 53.0 %all-to-all-start.1 = ((bf16[128,2,32,128]{0,3,1,2:T(8,128)(2,1)}), bf16[128,2,32,128]{0,3,1,2:T(8,128)(2,1)S(1)}, u32[]{:S(2)}, u32[]{:S(2)}) async-start(bf16[128,2,32,128]{0,3,1,2:T(8,128)(2,1)} %pad_maximum_fusion.1), calls=%async_computation.1 | async-start | bytes 4194304 | tf_op jit(solution)/shard_map/all_to_all | solution.py:88
  102.8 271.0 %all-gather.3.cloned.1.call-start = ((), (), s32[]{:S(2)}) async-start(), calls=%async_computation.10 | async-start | bytes 5242880 | tf_op jit(solution)/shard_map/all_gather | solution.py:66
  148.0 289.9 %reduce-scatter.5.cloned.1.call-start = ((), (), s32[]{:S(2)}) async-start(), calls=%async_computation.13 | async-start | bytes 5242880 | tf_op jit(solution)/shard_map/reduce_scatter | solution.py:43
  299.7 144.0 %all-gather.5.cloned.1.call-start = ((), (), s32[]{:S(2)}) async-start(), calls=%async_computation.11 | async-start | bytes 5242880 | tf_op jit(solution)/shard_map/all_gather | solution.py:66
  305.5 6.4 %collective-permute-start.1 = (f32[127,1,4096]{2,1,0:T(1,128)}, f32[127,1,4096]{2,1,0:T(1,128)}, u32[]{:S(2)}, u32[]{:S(2)}) collective-permute-start(f32[127,1,4096]{2,1,0:T(1,128)} %copy.107), channel_id=1, source_target_pairs={{1,0},{2,1},{3,2},{5,4},{6,5},{7,6},{9,8},{10,9},{11,10},{13,12},{... | collective-permute-start | bytes 6242312 | tf_op jit(solution)/shard_map/ppermute | solution.py:12
  317.5 3.7 copy-start.2
  329.1 101.5 %collective-permute-start.2 = (bf16[127,1,4096]{2,0,1:T(8,128)(2,1)}, bf16[127,1,4096]{2,0,1:T(8,128)(2,1)}, u32[]{:S(2)}, u32[]{:S(2)}) collective-permute-start(bf16[127,1,4096]{2,0,1:T(8,128)(2,1)} %slice.31), channel_id=1, source_target_pairs={{0,1},{1,2},{2,3},{4,5},{5,6},{6,7},{8,9},{9,10},{10,11},{12,13},{... | collective-permute-start | bytes 3121160 | tf_op jit(solution)/shard_map/ppermute | solution.py:12
  391.2 29.3 %all-to-all-start.4 = ((bf16[4,2,65536]{2,1,0:T(2,128)(2,1)}), bf16[4,2,65536]{2,1,0:T(2,128)(2,1)}, u32[]{:S(2)}, u32[]{:S(2)}) async-start(bf16[4,2,65536]{2,1,0:T(2,128)(2,1)} %reshape.476), calls=%async_computation.6 | async-start | bytes 2097152 | tf_op jit(solution)/shard_map/all_to_all | solution.py:72
  440.3 51.2 %collective-permute-start.3 = (bf16[127,1,4096]{2,0,1:T(8,128)(2,1)}, bf16[127,1,4096]{2,0,1:T(8,128)(2,1)}, u32[]{:S(2)}, u32[]{:S(2)}) collective-permute-start(bf16[127,1,4096]{2,0,1:T(8,128)(2,1)} %slice.32), channel_id=1, source_target_pairs={{0,1},{1,2},{2,3},{4,5},{5,6},{6,7},{8,9},{9,10},{10,11},{12,13},{... | collective-permute-start | bytes 3121160 | tf_op jit(solution)/shard_map/ppermute | solution.py:12
  460.9 20.5 %all-to-all-start.5 = ((bf16[4,2,65536]{2,1,0:T(2,128)(2,1)}), bf16[4,2,65536]{2,1,0:T(2,128)(2,1)}, u32[]{:S(2)}, u32[]{:S(2)}) async-start(bf16[4,2,65536]{2,1,0:T(2,128)(2,1)} %reshape.478), calls=%async_computation.7 | async-start | bytes 2097152 | tf_op jit(solution)/shard_map/all_to_all | solution.py:72
  498.8 5.3 copy-start.6
  506.3 4.8 copy-start.8
  506.3 22.8 %all-to-all-start.6 = ((bf16[128,1,32,128]{0,3,1,2:T(8,128)(2,1)}), bf16[128,1,32,128]{0,3,1,2:T(8,128)(2,1)}, u32[]{:S(2)}, u32[]{:S(2)}) async-start(bf16[128,1,32,128]{0,3,1,2:T(8,128)(2,1)} %bitcast.235), calls=%async_computation.8 | async-start | bytes 2097152 | tf_op jit(solution)/shard_map/all_to_all | solution.py:88
  514.9 22.0 %copy-start.15 = (bf16[4,128,1,1024]{3,1,0,2:T(8,128)(2,1)S(1)}, bf16[4,128,1,1024]{3,1,0,2:T(8,128)(2,1)}, u32[]{:S(2)}) copy-start(bf16[4,128,1,1024]{3,1,0,2:T(8,128)(2,1)} %copy-done.14) | copy-start | bytes 3145732
  514.9 53.1 %collective-permute-start.4 = (bf16[128,4096]{0,1:T(8,128)(2,1)}, bf16[128,4096]{0,1:T(8,128)(2,1)S(1)}, u32[]{:S(2)}, u32[]{:S(2)}) collective-permute-start(bf16[128,4096]{0,1:T(8,128)(2,1)} %fusion.51), channel_id=1, source_target_pairs={{4,0},{8,4},{12,8},{16,12},{20,16},{24,20},{28,24},{32,28},{36,32}... | collective-permute-start | bytes 3145736 | tf_op jit(solution)/shard_map/ppermute | solution.py:12
  531.4 39.9 %all-to-all-start.7 = ((bf16[128,1,32,128]{0,3,1,2:T(8,128)(2,1)}), bf16[128,1,32,128]{0,3,1,2:T(8,128)(2,1)S(1)}, u32[]{:S(2)}, u32[]{:S(2)}) async-start(bf16[128,1,32,128]{0,3,1,2:T(8,128)(2,1)} %rev.9), calls=%async_computation.9 | async-start | bytes 2097152 | tf_op jit(solution)/shard_map/all_to_all | solution.py:89
  536.9 10.6 %copy-start.7 = (bf16[255,1,4096]{0,2,1:T(8,128)(2,1)S(1)}, bf16[255,1,4096]{0,2,1:T(8,128)(2,1)}, u32[]{:S(2)}) copy-start(bf16[255,1,4096]{0,2,1:T(8,128)(2,1)} %copy.131) | copy-start | bytes 6266884
  536.9 10.5 %copy-start.11 = (f32[128,32,128]{2,0,1:T(8,128)S(1)}, f32[128,32,128]{2,0,1:T(8,128)}, u32[]{:S(2)}) copy-start(f32[128,32,128]{2,0,1:T(8,128)} %copy.111) | copy-start | bytes 6291460
  536.9 10.5 %copy-start.12 = (f32[128,32,128]{2,0,1:T(8,128)S(1)}, f32[128,32,128]{2,0,1:T(8,128)}, u32[]{:S(2)}) copy-start(f32[128,32,128]{2,0,1:T(8,128)} %copy.110) | copy-start | bytes 6291460
  568.0 1.0 copy-start.17
  569.0 8.6 %copy-start.16 = (bf16[4,128,1,1024]{3,1,0,2:T(8,128)(2,1)S(1)}, bf16[4,128,1,1024]{3,1,0,2:T(8,128)(2,1)}, u32[]{:S(2)}) copy-start(bf16[4,128,1,1024]{3,1,0,2:T(8,128)(2,1)} %copy.106) | copy-start | bytes 3145732
  572.6 16.3 %copy-start.5 = (f32[128,1,4096]{0,2,1:T(8,128)S(1)}, f32[128,1,4096]{0,2,1:T(8,128)}, u32[]{:S(2)}) copy-start(f32[128,1,4096]{0,2,1:T(8,128)} %get-tuple-element.20) | copy-start | bytes 6291460
  572.6 52.1 %collective-permute-start.5 = (bf16[128,4096]{1,0:T(8,128)(2,1)}, bf16[128,4096]{1,0:T(8,128)(2,1)}, u32[]{:S(2)}, u32[]{:S(2)}) collective-permute-start(bf16[128,4096]{1,0:T(8,128)(2,1)} %copy.126), channel_id=1, source_target_pairs={{0,4},{4,8},{8,12},{12,16},{16,20},{20,24},{24,28},{28,32},{32,36}... | collective-permute-start | bytes 3145736 | tf_op jit(solution)/shard_map/ppermute | solution.py:12
  599.8 27.2 %copy-start.1 = (f32[1,32,128]{2,1,0:T(8,128)S(1)}, f32[1,32,128]{2,1,0:T(8,128)}, u32[]{:S(2)}) copy-start(f32[1,32,128]{2,1,0:T(8,128)} %param.7) | copy-start | bytes 49156
Sparse Core Ops, SparseCore 0:
  75.3 83.9 reduce-scatter.2
  161.6 73.2 all-gather.2
  299.8 58.0 reduce-scatter.4
  359.4 49.8 all-gather.4
where the time goes:
time: 645 us; the launch traced here: 634 us
  matrix products  150 us (23%)
  local copies, waits for them, and re-layouts  149 us (23%)
  blocking collectives  118 us (18%)
  starting transfers between devices  95.3 us (15%)
  other arithmetic  81.4 us (13%)
  waiting for transfers between devices  25.4 us (4%)
  between operations  14.6 us (2%)
    all_to_all x2, blocking collectives, layer_grads(): lax.all_to_all(normed_b, 'tensor', split_axis=2, concat_axis=0, tiled=True)  77 us
    ppermute x6, starting transfers between devices, shifted(): return lax.ppermute(x, axis, pairs)  56.9 us
    unnamed x2, other arithmetic  47.8 us
    unnamed x53, local copies, waits for them, and re-layouts  46.8 us
    dot_general x2, matrix products, banded(): jnp.einsum('tuk,gk->gtu', table, filter_taps, precision=lax.Precision.HIG...  28 us
    dot_general x4, matrix products, banded(): jnp.einsum('gtu,umgc->tmgc', band, grouped, precision=lax.Precision.HIGHEST)  27.8 us
    all_to_all x1, blocking collectives, mirrored(): lax.all_to_all(jnp.flip(spread, 2), 'section', split_axis=2, concat_axis=...  27.6 us
    dot_general x2, matrix products, layer_grads(): jnp.einsum('gtu,tuk->gk', pairs, causal_table, precision=lax.Precision.HI...  22.3 us
  transfers between devices with their start and end apart: 15, of which 3 were waited for; matrix products, arithmetic and copies ran while one was open for 49% of the time, Pallas kernels for 0%

commit v1 on v0

--- a/solution.py
+++ b/solution.py
@@ -38,7 +38,12 @@
     inverse_rms = lax.rsqrt(jnp.mean(input_wide * input_wide, axis=2, keepdims=True) + epsilon)
     normed = input_wide * inverse_rms
     normed_b = normed.astype(jnp.bfloat16)
-    feature_rows = lax.all_to_all(normed_b, "tensor", split_axis=2, concat_axis=0, tiled=True)
+    feature_rows = jnp.concatenate(
+        lax.all_to_all(
+            jnp.stack(jnp.split(normed_b, lax.axis_size("tensor"), axis=2)), "tensor", 0, 0
+        ),
+        axis=0,
+    )
     selected = feature_rows
     values = lax.psum_scatter(
         jnp.einsum("tmd,de->tme", selected, weight_rows, preferred_element_type=jnp.float32).astype(

time: 645 us -> 545 us (0.84)
  other arithmetic: 81.4 us -> 35.9 us
  local copies, waits for them, and re-layouts: 149 us -> 123 us
  starting transfers between devices: 95.3 us -> 78.8 us
    unnamed x2, other arithmetic: 47.8 us -> 1.78 us
    convert_element_type x1, local copies, waits for them, and re-layouts: 17 us -> 0.51 us  [layer_grads(): returned_rows.astype(jnp.bfloat16)]
    unnamed x53 -> x50, local copies, waits for them, and re-layouts: 46.8 us -> 30.9 us
    ppermute x6, starting transfers between devices: 56.9 us -> 45.2 us  [shifted(): return lax.ppermute(x, axis, pairs)]
    all_gather x2, starting transfers between devices: 11.6 us -> 0.3 us  [layer_grads(): shard_rows = lax.all_gather(grad_values_b, 'tensor', axis=0, tiled=True)]
    another operation x3 -> x6, local copies, waits for them, and re-layouts: 9.45 us -> 13.3 us
    convert_element_type x2 -> x3, local copies, waits for them, and re-layouts: 12.2 us -> 15.1 us  [layer_grads(): back_tokens = lax.all_to_all(returned_rows.astype(jnp.bfloat16), 'tensor'...]
  transfers between devices with their start and end apart: 15 -> 15, of which waited for: 3 -> 4; matrix products, arithmetic and copies ran while one was open for 49% -> 50% of each run, Pallas kernels for 0% -> 0%
where the time goes in v1:
time: 545 us; the launch traced here: 536 us
  matrix products  147 us (27%)
  local copies, waits for them, and re-layouts  123 us (23%)
  blocking collectives  115 us (21%)
  starting transfers between devices  78.8 us (14%)
  other arithmetic  35.9 us (7%)
  waiting for transfers between devices  22.1 us (4%)
  between operations  14.7 us (3%)
    all_to_all x2, blocking collectives, layer_grads(): lax.all_to_all(jnp.stack(jnp.split(normed_b, lax.axis_size('tensor'), axi...  74 us
    ppermute x6, starting transfers between devices, shifted(): return lax.ppermute(x, axis, pairs)  45.2 us
    unnamed x50, local copies, waits for them, and re-layouts  30.9 us
    dot_general x2, matrix products, banded(): jnp.einsum('tuk,gk->gtu', table, filter_taps, precision=lax.Precision.HIG...  28 us
    all_to_all x1, blocking collectives, mirrored(): lax.all_to_all(jnp.flip(spread, 2), 'section', split_axis=2, concat_axis=...  27.4 us
    dot_general x4, matrix products, banded(): jnp.einsum('gtu,umgc->tmgc', band, grouped, precision=lax.Precision.HIGHEST)  27.2 us
    dot_general x2, matrix products, layer_grads(): jnp.einsum('gtu,tuk->gk', pairs, causal_table, precision=lax.Precision.HI...  22.3 us
    dot_general x2, matrix products, layer_grads(): jnp.einsum('tmd,tme->de', selected, shard_rows, preferred_element_type=jn...  21.9 us
  transfers between devices with their start and end apart: 15, of which 4 were waited for; matrix products, arithmetic and copies ran while one was open for 50% of the time, Pallas kernels for 0%

profile of v1, /device:TPU:0, one launch (start us, length us, event | category | flops | bytes accessed | tf_op | source)
XLA Modules:
  0.0 536.4 jit_solution(1531002002552755778)
XLA Ops:
  10.7 21.1 %all_to_all.48 = bf16[4,128,1,1024]{3,1,2,0:T(8,128)(2,1)S(1)} all-to-all(bf16[4,128,1,1024]{3,1,2,0:T(8,128)(2,1)S(1)} %pad_maximum_fusion.4), channel_id=1, replica_groups=mesh['section'=32,'tensor'=4] {'tensor'}, dimensions={0} | all-to-all | bytes 2097152 | tf_op jit(solution)/shard_map/all_to_all | solution.py:42
  32.8 6.1 %fusion.26 = bf16[512,1,4096]{2,0,1:T(8,128)(2,1)} fusion(bf16[512,1024]{1,0:T(8,128)(2,1)S(1)} %bitcast.240, bf16[1,1024,4096]{2,1,0:T(8,128)(2,1)S(1)} %copy-done.19), kind=kOutput, calls=%fused_computation.23 | convolution fusion | flops 4297064448 | bytes 13631488 | tf_op jit(solution)/shard_map/tmd,de->tme/dot_general | solution.py:49
  42.0 3.4 copy.77
  50.5 2.7 copy.82
  53.2 7.9 %all-to-all-start.1 = ((bf16[128,2,32,128]{3,0,1,2:T(8,128)(2,1)}), bf16[128,2,32,128]{3,0,1,2:T(8,128)(2,1)}, u32[]{:S(2)}, u32[]{:S(2)}) async-start(bf16[128,2,32,128]{3,0,1,2:T(8,128)(2,1)} %copy.82), calls=%async_computation.1 | async-start | bytes 4194304 | tf_op jit(solution)/shard_map/all_to_all | solution.py:93
  64.8 14.0 %fusion.40 = f32[32,128,255]{1,0,2:T(8,128)} fusion(s32[128,255]{0,1:T(8,128)S(1)} %iota_subtract_fusion.1, f32[1,32,128]{2,1,0:T(8,128)S(1)} %copy-done), kind=kOutput, calls=%fused_computation.42 | convolution fusion | flops 1608499200 | bytes 4324864 | tf_op jit(solution)/shard_map/tuk,gk->gtu/dot_general | solution.py:26
  78.8 5.2 copy.79
  84.1 3.3 multiply_multiply_fusion
  87.3 5.8 %copy.78 = f32[127,1,4096]{0,2,1:T(8,128)} copy(f32[127,1,4096]{2,1,0:T(1,128)} %collective-permute-done) | data formatting | bytes 4161536 | tf_op jit(solution)/shard_map/ppermute | solution.py:12
  93.1 8.0 %fusion.59 = bf16[32,128,128]{2,1,0:T(8,128)(2,1)} fusion(f32[32,128,255]{2,1,0:T(8,128)} %copy.79, f32[127,1,32,128]{0,3,2,1:T(8,128)} %bitcast.233, f32[128,1,32,128]{0,3,2,1:T(8,128)S(1)} %copy-done.10), kind=kOutput, calls=%fused_computation.76 | convolution fusion | flops 1605890048 | bytes 9404416 | tf_op jit(solution)/shard_map/gtu,umgc->tmgc/dot_general | solution.py:28
  103.0 27.4 %all_to_all.49 = bf16[128,2,32,128]{3,0,1,2:T(8,128)(2,1)} all-to-all(bf16[128,2,32,128]{3,0,1,2:T(8,128)(2,1)S(1)} %rev.8), channel_id=1, replica_groups=mesh['section'=32,'tensor'=4] {'section'}, dimensions={2} | all-to-all | bytes 4194304 | tf_op jit(solution)/shard_map/all_to_all | solution.py:94
  130.4 3.1 copy.83
  139.3 52.9 %all_to_all.50 = bf16[4,128,1,1024]{3,1,2,0:T(8,128)(2,1)S(1)} all-to-all(bf16[4,128,1,1024]{3,1,2,0:T(8,128)(2,1)} %copy.84), channel_id=1, replica_groups=mesh['section'=32,'tensor'=4] {'tensor'}, dimensions={0} | all-to-all | bytes 2097152 | tf_op jit(solution)/shard_map/all_to_all | solution.py:42
  193.2 9.5 %fusion.23 = bf16[512,1,4096]{2,0,1:T(8,128)(2,1)} fusion(bf16[512,1024]{1,0:T(8,128)(2,1)S(1)} %bitcast.242, bf16[1,1024,4096]{2,1,0:T(8,128)(2,1)} %param.6), kind=kOutput, calls=%fused_computation.22 | convolution fusion | flops 4297064448 | bytes 13631488 | tf_op jit(solution)/shard_map/tmd,de->tme/dot_general | solution.py:49
  202.7 5.7 %copy.85 = f32[127,1,4096]{2,1,0:T(1,128)} copy(f32[127,1,4096]{0,2,1:T(8,128)} %bitcast.218) | data formatting | bytes 4161536 | tf_op jit(solution)/shard_map/slice | solution.py:63
  210.1 4.8 collective-permute-done.1
  214.9 5.9 %copy.86 = f32[127,1,4096]{0,2,1:T(8,128)} copy(f32[127,1,4096]{2,1,0:T(1,128)} %collective-permute-done.1) | data formatting | bytes 4161536 | tf_op jit(solution)/shard_map/ppermute | solution.py:12
  220.8 2.7 pad_maximum_fusion
  224.2 5.2 convolution_convert_fusion
  229.5 2.5 slice.31
  232.0 32.7 %collective-permute-start.2 = (bf16[127,1,4096]{2,0,1:T(8,128)(2,1)}, bf16[127,1,4096]{2,0,1:T(8,128)(2,1)}, u32[]{:S(2)}, u32[]{:S(2)}) collective-permute-start(bf16[127,1,4096]{2,0,1:T(8,128)(2,1)} %slice.31), channel_id=1, source_target_pairs={{0,1},{1,2},{2,3},{4,5},{5,6},{6,7},{8,9},{9,10},{10,11},{12,13},{... | collective-permute-start | bytes 3121160 | tf_op jit(solution)/shard_map/ppermute | solution.py:12
  264.7 10.2 %fusion.75 = bf16[512,1,1024]{2,0,1:T(8,128)(2,1)} fusion(bf16[1,1024,4096]{2,1,0:T(8,128)(2,1)} %param.6, bf16[512,1,4096]{0,2,1:T(8,128)(2,1)} %all-gather.3.cloned.1.call-done), kind=kOutput, calls=%fused_computation.81 | convolution fusion | flops 4295491584 | bytes 13631488 | tf_op jit(solution)/shard_map/tme,de->tmd/dot_general | solution.py:74
  275.4 3.3 reduce.5
  278.7 3.7 reshape.474
  282.4 4.4 all-to-all-start.4
  286.9 14.0 %fusion.41 = f32[32,128,255]{1,0,2:T(8,128)} fusion(s32[128,255]{0,1:T(8,128)S(1)} %iota_subtract_fusion, f32[1,32,128]{2,1,0:T(8,128)S(1)} %copy-done), kind=kOutput, calls=%fused_computation.43 | convolution fusion | flops 1608499200 | bytes 4324864 | tf_op jit(solution)/shard_map/tuk,gk->gtu/dot_general | solution.py:26
  300.9 5.2 copy.96
  306.1 3.3 copy.112
  311.8 4.0 reshape.475
  315.7 6.1 %copy.99 = f32[4,128,1,1024]{1,3,0,2:T(8,128)} copy(bf16[4,128,1,1024]{3,2,1,0:T(2,128)(2,1)} %bitcast.229) | data formatting | bytes 3145728 | tf_op jit(solution)/shard_map/convert_element_type | solution.py:79
  321.8 2.9 copy.109
  324.7 3.2 pad_maximum_fusion.2
  327.9 4.1 copy.110
  332.0 2.4 slice.32
  334.5 2.9 collective-permute-start.3
  337.4 10.2 %fusion.70 = bf16[512,1,1024]{2,0,1:T(8,128)(2,1)} fusion(bf16[1,1024,4096]{2,1,0:T(8,128)(2,1)} %param.6, bf16[512,1,4096]{0,2,1:T(8,128)(2,1)} %all-gather.5.cloned.1.call-done), kind=kOutput, calls=%fused_computation.80 | convolution fusion | flops 4295491584 | bytes 13631488 | tf_op jit(solution)/shard_map/tme,de->tmd/dot_general | solution.py:74
  347.6 3.4 reduce.6
  351.0 3.7 reshape.476
  354.7 4.5 all-to-all-start.5
  359.2 8.6 %fusion.50 = (f32[128]{0:T(128)S(1)}, f32[32,128,128]{2,1,0:T(8,128)}) fusion(f32[128,1,32,128]{0,3,2,1:T(8,128)} %bitcast.225, f32[128,1,32,128]{0,3,2,1:T(8,128)} %bitcast.220, f32[128,1,32,128]{0,3,2,1:T(8,128)} %bitcast.221, f32[128]{0:T(128)S(1)} %add_rsqrt_fusion.1, bf16[255,32,128]{0,2,1:T(8,128)(2,1)} %bitcast.226, f32[32,128,255]{2,1,0:T(8,128)} %copy.96), kind=kOutput, calls=%fused_computation.57 | convolution fusion | flops 1606942592 | bytes 14656512 | tf_op jit(solution)/shard_map/gtu,umgc->tmgc/dot_general | solution.py:28
  367.8 2.9 copy.97
  370.7 4.5 all-to-all-done.5
  375.2 4.0 reshape.477
  379.2 6.1 %copy.104 = f32[4,128,1,1024]{1,3,0,2:T(8,128)} copy(bf16[4,128,1,1024]{3,2,1,0:T(2,128)(2,1)} %bitcast.230) | data formatting | bytes 3145728 | tf_op jit(solution)/shard_map/convert_element_type | solution.py:79
  385.3 3.3 pad_maximum_fusion.3
  388.6 4.1 copy.111
  392.7 5.3 fusion.90
  400.2 2.4 copy.105
  402.6 9.8 %all-to-all-start.6 = ((bf16[128,1,32,128]{3,0,1,2:T(8,128)(2,1)}), bf16[128,1,32,128]{3,0,1,2:T(8,128)(2,1)S(1)}, u32[]{:S(2)}, u32[]{:S(2)}) async-start(bf16[128,1,32,128]{3,0,1,2:T(8,128)(2,1)} %copy.105), calls=%async_computation.8 | async-start | bytes 2097152 | tf_op jit(solution)/shard_map/all_to_all | solution.py:93
  412.4 4.0 fusion.55
  417.8 12.3 %all-to-all-done.6 = bf16[128,1,32,128]{3,0,1,2:T(8,128)(2,1)S(1)} async-done(((bf16[128,1,32,128]{3,0,1,2:T(8,128)(2,1)}), bf16[128,1,32,128]{3,0,1,2:T(8,128)(2,1)S(1)}, u32[]{:S(2)}, u32[]{:S(2)}) %all-to-all-start.6) | async-done | bytes 1048608 | tf_op jit(solution)/shard_map/all_to_all | solution.py:93
  431.2 6.5 %all-to-all-start.7 = ((bf16[128,1,32,128]{3,0,1,2:T(8,128)(2,1)}), bf16[128,1,32,128]{3,0,1,2:T(8,128)(2,1)S(1)}, u32[]{:S(2)}, u32[]{:S(2)}) async-start(bf16[128,1,32,128]{3,0,1,2:T(8,128)(2,1)} %rev.9), calls=%async_computation.9 | async-start | bytes 2097152 | tf_op jit(solution)/shard_map/all_to_all | solution.py:94
  437.8 10.5 %fusion.35 = f32[1024,4096]{1,0:T(8,128)} fusion(bf16[512,1024]{1,0:T(8,128)(2,1)S(1)} %bitcast.241, bf16[512,1,4096]{0,2,1:T(8,128)(2,1)} %all-gather.3.cloned.1.call-done), kind=kOutput, calls=%fused_computation.32 | convolution fusion | flops 4294967296 | bytes 22020096 | tf_op jit(solution)/shard_map/tmd,tme->de/dot_general | solution.py:73
  448.3 6.1 %fusion.58 = f32[32,128,255]{2,1,0:T(8,128)} fusion(bf16[255,32,128]{0,2,1:T(8,128)(2,1)S(1)} %bitcast.227, f32[128,32,128]{2,1,0:T(8,128)S(1)} %bitcast.231, f32[128,32,128]{2,1,0:T(8,128)S(1)} %bitcast.232, f32[128]{0:T(128)S(1)} %add_rsqrt_fusion.1), kind=kOutput, calls=%fused_computation.70 | convolution fusion | flops 1605369856 | bytes 10461696 | tf_op jit(solution)/shard_map/tmgc,umgc->gtu/dot_general | solution.py:68
  454.4 5.4 %copy.91 = f32[32,128,255]{1,0,2:T(8,128)} copy(f32[32,128,255]{2,1,0:T(8,128)} %fusion.58) | data formatting | bytes 8355840 | tf_op jit(solution)/shard_map/tmgc,umgc->gtu/dot_general | solution.py:68
  459.8 11.2 %fusion.80 = f32[32,128]{1,0:T(8,128)S(1)} fusion(f32[32,128,255]{1,0,2:T(8,128)} %copy.91, s32[128,255]{0,1:T(8,128)S(1)} %iota_subtract_fusion), kind=kOutput, calls=%fused_computation.82 | convolution fusion | flops 1608499200 | bytes 4324864 | tf_op jit(solution)/shard_map/gtu,tuk->gk/dot_general | solution.py:69
  472.3 5.2 collective-permute-start.5
  477.6 11.4 %fusion.4 = bf16[1,1024,4096]{2,1,0:T(8,128)(2,1)} fusion(f32[1024,4096]{1,0:T(8,128)} %fusion.35, bf16[512,1024]{1,0:T(8,128)(2,1)S(1)} %bitcast.243, bf16[512,1,4096]{0,2,1:T(8,128)(2,1)} %all-gather.5.cloned.1.call-done), kind=kOutput, calls=%fused_computation.7 | convolution fusion | flops 4303355904 | bytes 30408704 | tf_op jit(solution)/shard_map/tmd,tme->de/dot_general | solution.py:73
  489.0 5.4 %fusion.89 = f32[32,128,255]{2,1,0:T(8,128)} fusion(f32[128,32,128]{0,2,1:T(8,128)S(1)} %bitcast.219, bf16[255,32,128]{0,2,1:T(8,128)(2,1)} %bitcast.223), kind=kOutput, calls=%fused_computation.108 | convolution fusion | flops 1604321280 | bytes 8364032 | tf_op jit(solution)/shard_map/tmgc,umgc->gtu/dot_general | solution.py:68
  494.4 5.5 %copy.94 = f32[32,128,255]{1,0,2:T(8,128)} copy(f32[32,128,255]{2,1,0:T(8,128)} %fusion.89) | data formatting | bytes 8355840 | tf_op jit(solution)/shard_map/tmgc,umgc->gtu/dot_general | solution.py:68
  499.9 11.2 %fusion.83 = f32[1,32,128]{2,1,0:T(8,128)S(1)} fusion(f32[32,128]{1,0:T(8,128)S(1)} %fusion.80, f32[32,128,255]{1,0,2:T(8,128)} %copy.94, s32[128,255]{0,1:T(8,128)S(1)} %iota_subtract_fusion), kind=kOutput, calls=%fused_computation.85 | convolution fusion | flops 1608503296 | bytes 4341248 | tf_op jit(solution)/shard_map/gtu,tuk->gk/dot_general | solution.py:69
  511.1 13.7 %psum.7 = f32[1,32,128]{2,1,0:T(8,128)} all-reduce(f32[1,32,128]{2,1,0:T(8,128)S(1)} %fusion.83), channel_id=1, replica_groups=mesh['section'=32,'tensor'=4] {'tensor'}, use_global_device_ids=true, to_apply=%region_4.5 | all-reduce | flops 4096 | bytes 32768 | tf_op jit(solution)/shard_map/psum | solution.py:118
  524.8 2.3 copy.107
  527.1 2.3 copy.123
  (94 shorter events, 36.3 us)
Async XLA Ops:
  7.2 57.7 %copy-start = (f32[1,32,128]{2,1,0:T(8,128)S(1)}, f32[1,32,128]{2,1,0:T(8,128)}, u32[]{:S(2)}) copy-start(f32[1,32,128]{2,1,0:T(8,128)} %param.7) | copy-start | bytes 49156
  7.2 222.3 %reduce-scatter.3.cloned.1.call-start = ((), (), s32[]{:S(2)}) async-start(), calls=%async_computation.12 | async-start | bytes 5242880 | tf_op jit(solution)/shard_map/reduce_scatter | solution.py:48
  8.8 24.1 %copy-start.19 = (bf16[1,1024,4096]{2,1,0:T(8,128)(2,1)S(1)}, bf16[1,1024,4096]{2,1,0:T(8,128)(2,1)}, u32[]{:S(2)}) copy-start(bf16[1,1024,4096]{2,1,0:T(8,128)(2,1)} %param.6) | copy-start | bytes 25165828
  31.9 1.0 copy-start.15
  38.9 1.2 copy-start.8
  42.0 4.8 copy-start.13
  42.0 5.4 %copy-start.14 = (bf16[1,128,4096]{2,1,0:T(8,128)(2,1)S(1)}, bf16[1,128,4096]{2,1,0:T(8,128)(2,1)}, u32[]{:S(2)}) copy-start(bf16[1,128,4096]{2,1,0:T(8,128)(2,1)} %param.11) | copy-start | bytes 3145732
  45.5 41.9 %collective-permute-start = (f32[127,1,4096]{2,1,0:T(1,128)}, f32[127,1,4096]{2,1,0:T(1,128)}, u32[]{:S(2)}, u32[]{:S(2)}) collective-permute-start(f32[127,1,4096]{2,1,0:T(1,128)} %copy.77), channel_id=1, source_target_pairs={{1,0},{2,1},{3,2},{5,4},{6,5},{7,6},{9,8},{10,9},{11,10},{13,12},{... | collective-permute-start | bytes 6242312 | tf_op jit(solution)/shard_map/ppermute | solution.py:12
  53.2 48.0 %all-to-all-start.1 = ((bf16[128,2,32,128]{3,0,1,2:T(8,128)(2,1)}), bf16[128,2,32,128]{3,0,1,2:T(8,128)(2,1)}, u32[]{:S(2)}, u32[]{:S(2)}) async-start(bf16[128,2,32,128]{3,0,1,2:T(8,128)(2,1)} %copy.82), calls=%async_computation.1 | async-start | bytes 4194304 | tf_op jit(solution)/shard_map/all_to_all | solution.py:93
  61.1 1.8 copy-start.4
  61.1 203.6 %all-gather.3.cloned.1.call-start = ((), (), s32[]{:S(2)}) async-start(), calls=%async_computation.10 | async-start | bytes 5242880 | tf_op jit(solution)/shard_map/all_gather | solution.py:71
  62.9 21.2 %copy-start.6 = (f32[1,128,4096]{1,2,0:T(8,128)}, f32[1,128,4096]{1,2,0:T(8,128)S(1)}, u32[]{:S(2)}) copy-start(f32[1,128,4096]{1,2,0:T(8,128)S(1)} %copy.75) | copy-start | bytes 6291460
  87.3 5.8 %copy-start.10 = (f32[128,1,32,128]{0,3,2,1:T(8,128)S(1)}, f32[128,1,32,128]{0,3,2,1:T(8,128)}, u32[]{:S(2)}) copy-start(f32[128,1,32,128]{0,3,2,1:T(8,128)} %multiply_multiply_fusion) | copy-start | bytes 6291460
  101.2 230.8 %reduce-scatter.5.cloned.1.call-start = ((), (), s32[]{:S(2)}) async-start(), calls=%async_computation.13 | async-start | bytes 5242880 | tf_op jit(solution)/shard_map/reduce_scatter | solution.py:48
  192.2 1.0 copy-start.17
  202.6 134.8 %all-gather.5.cloned.1.call-start = ((), (), s32[]{:S(2)}) async-start(), calls=%async_computation.11 | async-start | bytes 5242880 | tf_op jit(solution)/shard_map/all_gather | solution.py:71
  208.4 6.5 %collective-permute-start.1 = (f32[127,1,4096]{2,1,0:T(1,128)}, f32[127,1,4096]{2,1,0:T(1,128)}, u32[]{:S(2)}, u32[]{:S(2)}) collective-permute-start(f32[127,1,4096]{2,1,0:T(1,128)} %copy.85), channel_id=1, source_target_pairs={{1,0},{2,1},{3,2},{5,4},{6,5},{7,6},{9,8},{10,9},{11,10},{13,12},{... | collective-permute-start | bytes 6242312 | tf_op jit(solution)/shard_map/ppermute | solution.py:12
  220.8 3.4 copy-start.2
  232.0 92.7 %collective-permute-start.2 = (bf16[127,1,4096]{2,0,1:T(8,128)(2,1)}, bf16[127,1,4096]{2,0,1:T(8,128)(2,1)}, u32[]{:S(2)}, u32[]{:S(2)}) collective-permute-start(bf16[127,1,4096]{2,0,1:T(8,128)(2,1)} %slice.31), channel_id=1, source_target_pairs={{0,1},{1,2},{2,3},{4,5},{5,6},{6,7},{8,9},{9,10},{10,11},{12,13},{... | collective-permute-start | bytes 3121160 | tf_op jit(solution)/shard_map/ppermute | solution.py:12
  282.4 29.3 %all-to-all-start.4 = ((bf16[4,2,65536]{2,1,0:T(2,128)(2,1)}), bf16[4,2,65536]{2,1,0:T(2,128)(2,1)}, u32[]{:S(2)}, u32[]{:S(2)}) async-start(bf16[4,2,65536]{2,1,0:T(2,128)(2,1)} %reshape.474), calls=%async_computation.6 | async-start | bytes 2097152 | tf_op jit(solution)/shard_map/all_to_all | solution.py:77
  334.5 50.9 %collective-permute-start.3 = (bf16[127,1,4096]{2,0,1:T(8,128)(2,1)}, bf16[127,1,4096]{2,0,1:T(8,128)(2,1)}, u32[]{:S(2)}, u32[]{:S(2)}) collective-permute-start(bf16[127,1,4096]{2,0,1:T(8,128)(2,1)} %slice.32), channel_id=1, source_target_pairs={{0,1},{1,2},{2,3},{4,5},{5,6},{6,7},{8,9},{9,10},{10,11},{12,13},{... | collective-permute-start | bytes 3121160 | tf_op jit(solution)/shard_map/ppermute | solution.py:12
  354.7 20.5 %all-to-all-start.5 = ((bf16[4,2,65536]{2,1,0:T(2,128)(2,1)}), bf16[4,2,65536]{2,1,0:T(2,128)(2,1)}, u32[]{:S(2)}, u32[]{:S(2)}) async-start(bf16[4,2,65536]{2,1,0:T(2,128)(2,1)} %reshape.476), calls=%async_computation.7 | async-start | bytes 2097152 | tf_op jit(solution)/shard_map/all_to_all | solution.py:77
  392.7 5.3 copy-start.5
  400.2 12.2 %copy-start.9 = (bf16[1,128,4096]{2,1,0:T(8,128)(2,1)S(1)}, bf16[1,128,4096]{2,1,0:T(8,128)(2,1)}, u32[]{:S(2)}) copy-start(bf16[1,128,4096]{2,1,0:T(8,128)(2,1)} %param.9) | copy-start | bytes 3145732
  402.6 27.6 %all-to-all-start.6 = ((bf16[128,1,32,128]{3,0,1,2:T(8,128)(2,1)}), bf16[128,1,32,128]{3,0,1,2:T(8,128)(2,1)S(1)}, u32[]{:S(2)}, u32[]{:S(2)}) async-start(bf16[128,1,32,128]{3,0,1,2:T(8,128)(2,1)} %copy.105), calls=%async_computation.8 | async-start | bytes 2097152 | tf_op jit(solution)/shard_map/all_to_all | solution.py:93
  416.4 21.4 %copy-start.16 = (bf16[4,128,1,1024]{3,1,2,0:T(8,128)(2,1)S(1)}, bf16[4,128,1,1024]{3,1,2,0:T(8,128)(2,1)}, u32[]{:S(2)}) copy-start(bf16[4,128,1,1024]{3,1,2,0:T(8,128)(2,1)} %copy-done.15) | copy-start | bytes 3145732
  416.4 54.6 %collective-permute-start.4 = (bf16[128,4096]{1,0:T(8,128)(2,1)}, bf16[128,4096]{1,0:T(8,128)(2,1)}, u32[]{:S(2)}, u32[]{:S(2)}) collective-permute-start(bf16[128,4096]{1,0:T(8,128)(2,1)} %fusion.55), channel_id=1, source_target_pairs={{4,0},{8,4},{12,8},{16,12},{20,16},{24,20},{28,24},{32,28},{36,32}... | collective-permute-start | bytes 3145736 | tf_op jit(solution)/shard_map/ppermute | solution.py:12
  431.2 39.8 %all-to-all-start.7 = ((bf16[128,1,32,128]{3,0,1,2:T(8,128)(2,1)}), bf16[128,1,32,128]{3,0,1,2:T(8,128)(2,1)S(1)}, u32[]{:S(2)}, u32[]{:S(2)}) async-start(bf16[128,1,32,128]{3,0,1,2:T(8,128)(2,1)} %rev.9), calls=%async_computation.9 | async-start | bytes 2097152 | tf_op jit(solution)/shard_map/all_to_all | solution.py:94
  437.8 10.5 %copy-start.7 = (bf16[255,1,4096]{0,2,1:T(8,128)(2,1)S(1)}, bf16[255,1,4096]{0,2,1:T(8,128)(2,1)}, u32[]{:S(2)}) copy-start(bf16[255,1,4096]{0,2,1:T(8,128)(2,1)} %copy.110) | copy-start | bytes 6266884
  437.8 10.5 %copy-start.11 = (f32[16,8,32,128]{3,2,1,0:T(8,128)S(1)}, f32[16,8,32,128]{3,2,1,0:T(8,128)}, u32[]{:S(2)}) copy-start(f32[16,8,32,128]{3,2,1,0:T(8,128)} %copy.112) | copy-start | bytes 6291460
  437.8 10.5 %copy-start.12 = (f32[16,8,32,128]{3,2,1,0:T(8,128)S(1)}, f32[16,8,32,128]{3,2,1,0:T(8,128)}, u32[]{:S(2)}) copy-start(f32[16,8,32,128]{3,2,1,0:T(8,128)} %copy.113) | copy-start | bytes 6291460
  471.0 6.6 %copy-start.18 = (bf16[4,128,1,1024]{3,1,2,0:T(8,128)(2,1)S(1)}, bf16[4,128,1,1024]{3,1,2,0:T(8,128)(2,1)}, u32[]{:S(2)}) copy-start(bf16[4,128,1,1024]{3,1,2,0:T(8,128)(2,1)} %copy-done.17) | copy-start | bytes 3145732
  472.3 16.7 %copy-start.3 = (f32[128,1,4096]{0,2,1:T(8,128)S(1)}, f32[128,1,4096]{0,2,1:T(8,128)}, u32[]{:S(2)}) copy-start(f32[128,1,4096]{0,2,1:T(8,128)} %get-tuple-element.8) | copy-start | bytes 6291460
  472.3 52.4 %collective-permute-start.5 = (bf16[128,4096]{0,1:T(8,128)(2,1)}, bf16[128,4096]{0,1:T(8,128)(2,1)}, u32[]{:S(2)}, u32[]{:S(2)}) collective-permute-start(bf16[128,4096]{0,1:T(8,128)(2,1)} %bitcast.244), channel_id=1, source_target_pairs={{0,4},{4,8},{8,12},{12,16},{16,20},{20,24},{24,28},{28,32},{32,36}... | collective-permute-start | bytes 3145736 | tf_op jit(solution)/shard_map/ppermute | solution.py:12
  524.8 4.6 copy-start.1
Sparse Core Ops, SparseCore 0:
  39.1 92.4 reduce-scatter.2
  133.9 51.4 all-gather.2
  202.8 59.4 reduce-scatter.4
  263.7 47.7 all-gather.4
